TPU v7x, 128 devices: a whole 4x4x4 slice. The times are simulated.
128 devices in a mesh: blk: 16 (over y, z), order: 8 (over x, core).
Axes of the slice: x: 4, y: 4, z: 4, core: 2. Of those that a mesh axis runs over, the one named last changes fastest.
Arguments:
- harmonics: float32 [128, 4, 8192], P('order', None, 'blk'), may hold values from -6 to 6
- legendre: float32 [128, 2, 256, 8192], P('order', None, 'blk'), may hold values from -0.005859375 to 0.005859375
- sky_map: float32 [256, 2, 16384], P(('blk', 'order')), may hold values from -6 to 6
- cycle_length: int32 [256], P(('blk', 'order')), may hold values from 4 to 16384, as said below
- cycle_offset: int32 [256], P(('blk', 'order')), may hold values from 0 to 1, as said below
- cycle_weight: float32 [256], P(('blk', 'order')), may hold values from 0.1 to 0.4
- order_ids: int32 [128], P('order'), may hold values from 0 to 8191, as said below
Outputs:
- refined: float32 [128, 4, 8192], P('order', None, 'blk')
- residual: float32 [256, 2, 16384], P(('blk', 'order'))
Inputs may be any that keep to these rules, and one draw needn't show every extreme that they name: `cycle_length`: cycle lengths are multiples of 4. Of each device's 2 consecutive cycles, those at even places have 4 * 4096 pixels, those at odd places 4 j pixels for some j from 1 to 4095. `cycle_offset`: 1 on every cycle of fewer than 16384 pixels. `order_ids`: the orders are distinct; 0 and 8191 are among them. Slot s (from 0) of each index of order holds an order from s * 512 to (s + 1) * 512 - 1.
All inputs are finite; a program needn't handle non-finite values.
Results may differ from a plain program's by a relative error of at most 0.0003.
Values sent between devices are 32-bit elements; how exact they have to be, the bound alone decides.
A program may use at most 192 MiB of HBM per device.

v0:
```python
import math

import jax
import jax.numpy as jnp
from jax import lax
from jax.sharding import PartitionSpec as P

HIGHEST = lax.Precision.HIGHEST


def cycle_tables(orders, length, offset, first_pixel, block_width):
    pixels = first_pixel + lax.iota(jnp.int32, block_width)
    phase_turns = orders[:, None] * (2 * pixels + offset)[None, :] % (2 * length)
    angles = phase_turns.astype(jnp.float32) * (math.pi / length.astype(jnp.float32))
    inside = (pixels < length).astype(jnp.float32)
    return (jnp.concatenate([jnp.cos(angles), jnp.sin(angles)], axis=0), inside)


def synth_weights(phases, factor):
    scaled = phases * factor[:, None]
    first_row = jnp.concatenate([scaled[:, 0], -scaled[:, 1]])
    second_row = jnp.concatenate([scaled[:, 2], -scaled[:, 3]])
    return jnp.stack([first_row, second_row])


def fold_totals(totals, weighting):
    half = totals.shape[1] // 2
    return weighting * jnp.stack(
        [totals[0, :half], -totals[0, half:], totals[1, :half], -totals[1, half:]], axis=1
    )


def assemble(products):
    positive = products[:, 0]
    negative = products[:, 1]
    return jnp.stack(
        [
            -positive[:, 0] + negative[:, 3],
            -positive[:, 1] - negative[:, 2],
            -positive[:, 2] - negative[:, 1],
            -positive[:, 3] + negative[:, 0],
        ],
        axis=1,
    )


def adjoint_coeffs(returned):
    positive = -returned
    negative = jnp.stack([returned[:, 3], -returned[:, 2], -returned[:, 1], returned[:, 0]], axis=1)
    return jnp.stack([positive, negative], axis=1)


def block_count(padded_length, block_width):
    return padded_length // block_width


def owner_cycle(inputs, orders, factor, normalise, block_width):
    cycle_phases, sky_row, length, offset, weight = inputs
    padded_length = sky_row.shape[1]
    weights = synth_weights(cycle_phases, factor)

    def advance(block_index, state_pair):
        residual, totals = state_pair
        first_pixel = block_index * block_width
        trig_table, inside = cycle_tables(orders, length, offset, first_pixel, block_width)
        modelled = jnp.dot(weights, trig_table, precision=HIGHEST)
        observed = lax.dynamic_slice_in_dim(sky_row, first_pixel, block_width, 1)
        section = (observed - modelled) * inside[None, :]
        residual = lax.dynamic_update_slice_in_dim(residual, section, first_pixel, 1)
        totals = totals + lax.dot_general(
            section, trig_table, (((1,), (1,)), ((), ())), precision=HIGHEST
        )
        return (residual, totals)

    start_state = (jnp.zeros_like(sky_row), jnp.zeros((2, weights.shape[1]), jnp.float32))
    residual, totals = lax.fori_loop(
        0, block_count(padded_length, block_width), advance, start_state
    )
    return (residual, fold_totals(totals, weight * normalise))


def body(harmonics, legendre, sky_map, cycle_length, cycle_offset, cycle_weight, order_ids):
    order_size = lax.axis_size("order")
    blk_size = lax.axis_size("blk")
    local_orders = order_ids.shape[0]
    ell_count = legendre.shape[3]
    padded_length = sky_map.shape[2]
    block_width = min(2048, padded_length)
    cycle_total = cycle_length.shape[0] * order_size * blk_size
    normalise = math.sqrt(ell_count * local_orders * order_size / (cycle_total * padded_length))
    floors = jnp.maximum(order_ids, 2)
    section = lax.all_gather(harmonics, "blk", axis=2, tiled=True)
    section_width = section.shape[2]
    degrees = lax.iota(jnp.int32, section_width)
    keep_mask = (degrees[None, :] >= floors[:, None]).astype(jnp.float32)
    products = jnp.einsum(
        "mtrl,mcl->mtcr", legendre, section * keep_mask[:, None, :], precision=HIGHEST
    )
    phases = assemble(products)
    all_orders = lax.all_gather(order_ids, "order", axis=0, tiled=True)
    factor = jnp.where(all_orders == 0, 1.0, 2.0).astype(jnp.float32)
    cycle_phases = lax.all_to_all(phases, "order", split_axis=2, concat_axis=0, tiled=True)

    def one_cycle(inputs):
        return owner_cycle(inputs, all_orders, factor, normalise, block_width)

    residual, analysed = lax.map(
        one_cycle,
        (jnp.transpose(cycle_phases, (2, 0, 1)), sky_map, cycle_length, cycle_offset, cycle_weight),
    )
    returned = lax.all_to_all(
        jnp.transpose(analysed, (1, 2, 0)), "order", split_axis=0, concat_axis=2, tiled=True
    )
    coeffs = adjoint_coeffs(returned)
    shard_width = harmonics.shape[2]
    update = jnp.einsum("mtrl,mtar->mal", legendre, coeffs, precision=HIGHEST)
    own_update = lax.psum_scatter(update, "blk", scatter_dimension=2, tiled=True)
    degrees = lax.axis_index("blk") * shard_width + lax.iota(jnp.int32, shard_width)
    valid_mask = (degrees[None, :] >= floors[:, None]).astype(jnp.float32)
    refined = valid_mask[:, None, :] * (harmonics + own_update)
    return (refined, residual)


def solution(mesh):
    return jax.shard_map(
        body,
        mesh=mesh,
        in_specs=(
            P("order", None, "blk"),
            P("order", None, "blk", None),
            P(("blk", "order"), None, None),
            P(("blk", "order")),
            P(("blk", "order")),
            P(("blk", "order")),
            P("order"),
        ),
        out_specs=(P("order", None, "blk"), P(("blk", "order"), None, None)),
        check_vma=False,
    )
```

profile of v0, /device:TPU:0, one launch (start us, length us, event | category | flops | bytes accessed | tf_op | source)
XLA Modules:
  0.0 618.2 jit_solution(3518168744225803581)
XLA Ops:
  20.8 38.9 %all-gather.2.cloned.1.call-done = f32[16,4,8192]{2,1,0:T(4,128)} async-done(((f32[16,4,512]{2,1,0:T(4,128)}), f32[16,4,8192]{2,1,0:T(4,128)}) %all-gather.2.cloned.1.call-update) | async-done | bytes 2097168 | tf_op jit(solution)/shard_map/all_gather | solution.py:92
  59.8 61.1 %fusion.20 = f32[16,2,4,16]{3,2,1,0:T(4,128)S(1)} fusion(f32[16,2,16,8192]{3,2,1,0:T(8,128)} %param.12, f32[16,4,8192]{2,1,0:T(4,128)} %all-gather.2.cloned.1.call-done, f32[16,8192]{1,0:T(8,128)S(1)} %fusion.24), kind=kOutput, calls=%fused_computation.44 | convolution fusion | flops 201850880 | bytes 19406848 | tf_op jit(solution)/shard_map/mtrl,mcl->mtcr/dot_general | solution.py:96
  132.7 295.9 %while.31 = (s32[]{:T(128)}, f32[2,2,16384]{2,1,0:T(2,128)S(1)}, f32[2,128,4]{1,2,0:T(4,128)S(1)}, s32[2]{0:T(128)S(1)}, s32[2]{0:T(128)S(1)}, /*index=5*/f32[2,...) while((s32[]{:T(128)}, f32[2,2,16384]{2,1,0:T(2,128)S(1)}, ...), condition=%wide.region_3.4_spmd, body=%wide.region_0.3_spmd.sunk | while | flops 28861456 | bytes 7081630 | solution.py:107
  135.5 143.7 %while.32 = (s32[]{:T(128)}, f32[2,16384]{1,0:T(2,128)S(1)}, f32[2,256]{1,0:T(2,128)S(1)}, f32[2,16384]{1,0:T(2,128)S(1)}, s32[128]{0:T(128)S(1)}, /*index=5*/s3...) while((s32[]{:T(128)}, f32[2,16384]{1,0:T(2,128)S(1)}, ...), condition=%wide.region_2.2_spmd.clone, body=%wide.region_1.1_spmd.clone.sunk | while | flops 28857352 | bytes 6396642 | solution.py:76
  136.1 13.8 %fusion.44 = (f32[128,2048]{1,0:T(8,128)S(1)}, f32[128,2048]{1,0:T(8,128)S(1)}) fusion(f32[]{:T(128)} %get-tuple-element.619, s32[]{:T(128)} %get-tuple-element.617, s32[2048]{0:T(1024)S(1)} %multiply_add_fusion.2, s32[128]{0:T(128)S(1)} %get-tuple-element.615, pred[]{:T(512)} %get-tuple-element.618), kind=kLoop, calls=%fused_computation.13.clone.1 | loop fusion | flops 2621440 | bytes 2105865 | tf_op jit(solution)/shard_map/while/body/eval_jaxpr/while/body/eval_jaxpr/cos | solution.py:16
  154.1 13.8 %fusion.44 = (f32[128,2048]{1,0:T(8,128)S(1)}, f32[128,2048]{1,0:T(8,128)S(1)}) fusion(f32[]{:T(128)} %get-tuple-element.619, s32[]{:T(128)} %get-tuple-element.617, s32[2048]{0:T(1024)S(1)} %multiply_add_fusion.2, s32[128]{0:T(128)S(1)} %get-tuple-element.615, pred[]{:T(512)} %get-tuple-element.618), kind=kLoop, calls=%fused_computation.13.clone.1 | loop fusion | flops 2621440 | bytes 2105865 | tf_op jit(solution)/shard_map/while/body/eval_jaxpr/while/body/eval_jaxpr/cos | solution.py:16
  172.0 13.8 %fusion.44 = (f32[128,2048]{1,0:T(8,128)S(1)}, f32[128,2048]{1,0:T(8,128)S(1)}) fusion(f32[]{:T(128)} %get-tuple-element.619, s32[]{:T(128)} %get-tuple-element.617, s32[2048]{0:T(1024)S(1)} %multiply_add_fusion.2, s32[128]{0:T(128)S(1)} %get-tuple-element.615, pred[]{:T(512)} %get-tuple-element.618), kind=kLoop, calls=%fused_computation.13.clone.1 | loop fusion | flops 2621440 | bytes 2105865 | tf_op jit(solution)/shard_map/while/body/eval_jaxpr/while/body/eval_jaxpr/cos | solution.py:16
  190.0 13.8 %fusion.44 = (f32[128,2048]{1,0:T(8,128)S(1)}, f32[128,2048]{1,0:T(8,128)S(1)}) fusion(f32[]{:T(128)} %get-tuple-element.619, s32[]{:T(128)} %get-tuple-element.617, s32[2048]{0:T(1024)S(1)} %multiply_add_fusion.2, s32[128]{0:T(128)S(1)} %get-tuple-element.615, pred[]{:T(512)} %get-tuple-element.618), kind=kLoop, calls=%fused_computation.13.clone.1 | loop fusion | flops 2621440 | bytes 2105865 | tf_op jit(solution)/shard_map/while/body/eval_jaxpr/while/body/eval_jaxpr/cos | solution.py:16
  208.0 13.8 %fusion.44 = (f32[128,2048]{1,0:T(8,128)S(1)}, f32[128,2048]{1,0:T(8,128)S(1)}) fusion(f32[]{:T(128)} %get-tuple-element.619, s32[]{:T(128)} %get-tuple-element.617, s32[2048]{0:T(1024)S(1)} %multiply_add_fusion.2, s32[128]{0:T(128)S(1)} %get-tuple-element.615, pred[]{:T(512)} %get-tuple-element.618), kind=kLoop, calls=%fused_computation.13.clone.1 | loop fusion | flops 2621440 | bytes 2105865 | tf_op jit(solution)/shard_map/while/body/eval_jaxpr/while/body/eval_jaxpr/cos | solution.py:16
  225.9 13.8 %fusion.44 = (f32[128,2048]{1,0:T(8,128)S(1)}, f32[128,2048]{1,0:T(8,128)S(1)}) fusion(f32[]{:T(128)} %get-tuple-element.619, s32[]{:T(128)} %get-tuple-element.617, s32[2048]{0:T(1024)S(1)} %multiply_add_fusion.2, s32[128]{0:T(128)S(1)} %get-tuple-element.615, pred[]{:T(512)} %get-tuple-element.618), kind=kLoop, calls=%fused_computation.13.clone.1 | loop fusion | flops 2621440 | bytes 2105865 | tf_op jit(solution)/shard_map/while/body/eval_jaxpr/while/body/eval_jaxpr/cos | solution.py:16
  243.9 13.8 %fusion.44 = (f32[128,2048]{1,0:T(8,128)S(1)}, f32[128,2048]{1,0:T(8,128)S(1)}) fusion(f32[]{:T(128)} %get-tuple-element.619, s32[]{:T(128)} %get-tuple-element.617, s32[2048]{0:T(1024)S(1)} %multiply_add_fusion.2, s32[128]{0:T(128)S(1)} %get-tuple-element.615, pred[]{:T(512)} %get-tuple-element.618), kind=kLoop, calls=%fused_computation.13.clone.1 | loop fusion | flops 2621440 | bytes 2105865 | tf_op jit(solution)/shard_map/while/body/eval_jaxpr/while/body/eval_jaxpr/cos | solution.py:16
  261.9 13.8 %fusion.44 = (f32[128,2048]{1,0:T(8,128)S(1)}, f32[128,2048]{1,0:T(8,128)S(1)}) fusion(f32[]{:T(128)} %get-tuple-element.619, s32[]{:T(128)} %get-tuple-element.617, s32[2048]{0:T(1024)S(1)} %multiply_add_fusion.2, s32[128]{0:T(128)S(1)} %get-tuple-element.615, pred[]{:T(512)} %get-tuple-element.618), kind=kLoop, calls=%fused_computation.13.clone.1 | loop fusion | flops 2621440 | bytes 2105865 | tf_op jit(solution)/shard_map/while/body/eval_jaxpr/while/body/eval_jaxpr/cos | solution.py:16
  283.2 143.7 %while.32 = (s32[]{:T(128)}, f32[2,16384]{1,0:T(2,128)S(1)}, f32[2,256]{1,0:T(2,128)S(1)}, f32[2,16384]{1,0:T(2,128)S(1)}, s32[128]{0:T(128)S(1)}, /*index=5*/s3...) while((s32[]{:T(128)}, f32[2,16384]{1,0:T(2,128)S(1)}, ...), condition=%wide.region_2.2_spmd.clone, body=%wide.region_1.1_spmd.clone.sunk | while | flops 28857352 | bytes 6396642 | solution.py:76
  283.8 13.8 %fusion.44 = (f32[128,2048]{1,0:T(8,128)S(1)}, f32[128,2048]{1,0:T(8,128)S(1)}) fusion(f32[]{:T(128)} %get-tuple-element.619, s32[]{:T(128)} %get-tuple-element.617, s32[2048]{0:T(1024)S(1)} %multiply_add_fusion.2, s32[128]{0:T(128)S(1)} %get-tuple-element.615, pred[]{:T(512)} %get-tuple-element.618), kind=kLoop, calls=%fused_computation.13.clone.1 | loop fusion | flops 2621440 | bytes 2105865 | tf_op jit(solution)/shard_map/while/body/eval_jaxpr/while/body/eval_jaxpr/cos | solution.py:16
  301.8 13.8 %fusion.44 = (f32[128,2048]{1,0:T(8,128)S(1)}, f32[128,2048]{1,0:T(8,128)S(1)}) fusion(f32[]{:T(128)} %get-tuple-element.619, s32[]{:T(128)} %get-tuple-element.617, s32[2048]{0:T(1024)S(1)} %multiply_add_fusion.2, s32[128]{0:T(128)S(1)} %get-tuple-element.615, pred[]{:T(512)} %get-tuple-element.618), kind=kLoop, calls=%fused_computation.13.clone.1 | loop fusion | flops 2621440 | bytes 2105865 | tf_op jit(solution)/shard_map/while/body/eval_jaxpr/while/body/eval_jaxpr/cos | solution.py:16
  319.8 13.8 %fusion.44 = (f32[128,2048]{1,0:T(8,128)S(1)}, f32[128,2048]{1,0:T(8,128)S(1)}) fusion(f32[]{:T(128)} %get-tuple-element.619, s32[]{:T(128)} %get-tuple-element.617, s32[2048]{0:T(1024)S(1)} %multiply_add_fusion.2, s32[128]{0:T(128)S(1)} %get-tuple-element.615, pred[]{:T(512)} %get-tuple-element.618), kind=kLoop, calls=%fused_computation.13.clone.1 | loop fusion | flops 2621440 | bytes 2105865 | tf_op jit(solution)/shard_map/while/body/eval_jaxpr/while/body/eval_jaxpr/cos | solution.py:16
  337.7 13.8 %fusion.44 = (f32[128,2048]{1,0:T(8,128)S(1)}, f32[128,2048]{1,0:T(8,128)S(1)}) fusion(f32[]{:T(128)} %get-tuple-element.619, s32[]{:T(128)} %get-tuple-element.617, s32[2048]{0:T(1024)S(1)} %multiply_add_fusion.2, s32[128]{0:T(128)S(1)} %get-tuple-element.615, pred[]{:T(512)} %get-tuple-element.618), kind=kLoop, calls=%fused_computation.13.clone.1 | loop fusion | flops 2621440 | bytes 2105865 | tf_op jit(solution)/shard_map/while/body/eval_jaxpr/while/body/eval_jaxpr/cos | solution.py:16
  355.7 13.8 %fusion.44 = (f32[128,2048]{1,0:T(8,128)S(1)}, f32[128,2048]{1,0:T(8,128)S(1)}) fusion(f32[]{:T(128)} %get-tuple-element.619, s32[]{:T(128)} %get-tuple-element.617, s32[2048]{0:T(1024)S(1)} %multiply_add_fusion.2, s32[128]{0:T(128)S(1)} %get-tuple-element.615, pred[]{:T(512)} %get-tuple-element.618), kind=kLoop, calls=%fused_computation.13.clone.1 | loop fusion | flops 2621440 | bytes 2105865 | tf_op jit(solution)/shard_map/while/body/eval_jaxpr/while/body/eval_jaxpr/cos | solution.py:16
  373.7 13.8 %fusion.44 = (f32[128,2048]{1,0:T(8,128)S(1)}, f32[128,2048]{1,0:T(8,128)S(1)}) fusion(f32[]{:T(128)} %get-tuple-element.619, s32[]{:T(128)} %get-tuple-element.617, s32[2048]{0:T(1024)S(1)} %multiply_add_fusion.2, s32[128]{0:T(128)S(1)} %get-tuple-element.615, pred[]{:T(512)} %get-tuple-element.618), kind=kLoop, calls=%fused_computation.13.clone.1 | loop fusion | flops 2621440 | bytes 2105865 | tf_op jit(solution)/shard_map/while/body/eval_jaxpr/while/body/eval_jaxpr/cos | solution.py:16
  391.6 13.8 %fusion.44 = (f32[128,2048]{1,0:T(8,128)S(1)}, f32[128,2048]{1,0:T(8,128)S(1)}) fusion(f32[]{:T(128)} %get-tuple-element.619, s32[]{:T(128)} %get-tuple-element.617, s32[2048]{0:T(1024)S(1)} %multiply_add_fusion.2, s32[128]{0:T(128)S(1)} %get-tuple-element.615, pred[]{:T(512)} %get-tuple-element.618), kind=kLoop, calls=%fused_computation.13.clone.1 | loop fusion | flops 2621440 | bytes 2105865 | tf_op jit(solution)/shard_map/while/body/eval_jaxpr/while/body/eval_jaxpr/cos | solution.py:16
  409.6 13.8 %fusion.44 = (f32[128,2048]{1,0:T(8,128)S(1)}, f32[128,2048]{1,0:T(8,128)S(1)}) fusion(f32[]{:T(128)} %get-tuple-element.619, s32[]{:T(128)} %get-tuple-element.617, s32[2048]{0:T(1024)S(1)} %multiply_add_fusion.2, s32[128]{0:T(128)S(1)} %get-tuple-element.615, pred[]{:T(512)} %get-tuple-element.618), kind=kLoop, calls=%fused_computation.13.clone.1 | loop fusion | flops 2621440 | bytes 2105865 | tf_op jit(solution)/shard_map/while/body/eval_jaxpr/while/body/eval_jaxpr/cos | solution.py:16
  449.4 31.5 %copy.56 = f32[16,4,8192]{1,0,2:T(8,128)} copy(f32[16,4,8192]{2,1,0:T(4,128)S(1)} %convolution_bitcast_fusion.1) | data formatting | bytes 4194304
  480.8 46.1 %reshape.163 = f32[8192,64]{1,0:T(8,128)} reshape(f32[8192,16,4]{2,1,0:T(8,128)} %bitcast.35) | data formatting | bytes 4194304
  527.0 76.2 %reduce-scatter.4.cloned.1.call-done = f32[512,64]{1,0:T(8,128)} async-done(((f32[8192,64]{1,0:T(8,128)}), f32[512,64]{1,0:T(8,128)}) %reduce-scatter.4.cloned.1.call-update) | async-done | bytes 131088
  (153 shorter events, 124.1 us)
Async XLA Ops:
  7.2 52.6 %all-gather.2.cloned.1.call-start = ((), (), s32[]{:S(2)}) async-start(), calls=%async_computation.3 | async-start | bytes 2228224 | tf_op jit(solution)/shard_map/all_gather | solution.py:92
  20.8 111.8 %copy-start = (f32[2,2,16384]{2,1,0:T(2,128)S(1)}, f32[2,2,16384]{2,1,0:T(2,128)}, u32[]{:S(2)}) copy-start(f32[2,2,16384]{2,1,0:T(2,128)} %param.13) | copy-start | bytes 786436
  20.8 111.8 %copy-start.3 = (s32[2]{0:T(128)S(1)}, s32[2]{0:T(128)}, u32[]{:S(2)}) copy-start(s32[2]{0:T(128)} %param.15) | copy-start | bytes 28
  20.8 111.8 %copy-start.4 = (s32[2]{0:T(128)S(1)}, s32[2]{0:T(128)}, u32[]{:S(2)}) copy-start(s32[2]{0:T(128)} %param.14) | copy-start | bytes 28
  20.8 111.8 %copy-start.5 = (f32[2]{0:T(128)S(1)}, f32[2]{0:T(128)}, u32[]{:S(2)}) copy-start(f32[2]{0:T(128)} %param.16) | copy-start | bytes 28
  121.8 9.5 %all-to-all-start = ((f32[8,1,128]{2,1,0:T(1,128)}), f32[8,1,128]{2,1,0:T(1,128)S(1)}, u32[]{:S(2)}, u32[]{:S(2)}) async-start(f32[8,1,128]{2,1,0:T(1,128)} %reshape.165), calls=%async_computation | async-start | bytes 8192 | tf_op jit(solution)/shard_map/all_to_all | solution.py:102
  126.0 477.3 %reduce-scatter.4.cloned.1.call-start = ((), (), s32[]{:S(2)}) async-start(), calls=%async_computation.4 | async-start | bytes 4456448
  428.5 20.8 %copy-start.2 = (f32[2,2,16384]{2,1,0:T(2,128)}, f32[2,2,16384]{2,1,0:T(2,128)S(1)}, u32[]{:S(2)}) copy-start(f32[2,2,16384]{2,1,0:T(2,128)S(1)} %get-tuple-element.263) | copy-start | bytes 786436
  607.8 2.9 copy-start.1
Sparse Core Ops, SparseCore 0:
  10.1 49.6 all-gather.1
  527.1 76.1 reduce-scatter.3
where the time goes:
time: 620 us; the launch traced here: 618 us
  other arithmetic  243 us (39%)
  waiting for transfers between devices  121 us (20%)
  matrix products  119 us (19%)
  local copies, waits for them, and re-layouts  93.5 us (15%)
  blocking collectives  17 us (3%)
  between operations  15 us (2%)
    cos x16, other arithmetic, cycle_tables(): return (jnp.concatenate([jnp.cos(angles), jnp.sin(angles)], axis=0), inside)  221 us
    unnamed x28, local copies, waits for them, and re-layouts  88.6 us
    unnamed x3, waiting for transfers between devices  76.9 us
    dot_general x1, matrix products, body(): jnp.einsum('mtrl,mcl->mtcr', legendre, section * keep_mask[:, None, :], p...  61.1 us
    all_gather x1, waiting for transfers between devices, body(): section = lax.all_gather(harmonics, 'blk', axis=2, tiled=True)  38.9 us
    dot_general x16, matrix products, advance(): lax.dot_general(section, trig_table, (((1,), (1,)), ((), ())), precision=...  27.8 us
    dot_general x16, matrix products, advance(): modelled = jnp.dot(weights, trig_table, precision=HIGHEST)  19.2 us
  transfers between devices with their start and end apart: 3, of which 3 were waited for; matrix products, arithmetic and copies ran while one was open for 0% of the time, Pallas kernels for 0%

commit v1 on v0

v1 whole, which is shorter than its diff:
```python
import functools
import math

import jax
import jax.numpy as jnp
from jax import lax
from jax.experimental import pallas as pl
from jax.experimental.pallas import tpu as pltpu
from jax.sharding import PartitionSpec as P

HIGHEST = lax.Precision.HIGHEST
F32 = jnp.float32
SLOTS = 16
BLOCKS = 16
WIDTH = 512
GROUP = 8
LANES = 128
VMEM_LIMIT = 60 * 1024 * 1024


def lane_iota(shape):
    return lax.broadcasted_iota(jnp.int32, shape, len(shape) - 1)


def row_iota(shape):
    return lax.broadcasted_iota(jnp.int32, shape, 0)


def table_copies(leg_ref, tables, sems):
    copies = []
    for s in range(SLOTS):
        cut = pl.ds(s * WIDTH, (BLOCKS - s) * WIDTH)
        copies.append(
            pltpu.make_async_copy(
                leg_ref.at[s, :, :, cut], tables.at[s, :, :, cut], sems.at[s]
            )
        )
    return copies


def forward_column(accs, tables, gathered, s, b, j, keep=None):
    lanes = pl.ds(pl.multiple_of(b * WIDTH + j * LANES, LANES), LANES)
    values = [
        jnp.broadcast_to(gathered[b, s, a : a + 1, j * LANES : (j + 1) * LANES], (8, LANES))
        for a in range(4)
    ]
    if keep is not None:
        values = [jnp.where(keep, v, 0.0) for v in values]
    out = []
    for half in range(2):
        plus = tables[s, 0, half * 8 : half * 8 + 8, lanes]
        minus = tables[s, 1, half * 8 : half * 8 + 8, lanes]
        a0, a1, a2, a3 = accs[half * 4 : half * 4 + 4]
        out += [
            a0 + (minus * values[3] - plus * values[0]),
            a1 - (plus * values[1] + minus * values[2]),
            a2 - (plus * values[2] + minus * values[1]),
            a3 + (minus * values[0] - plus * values[3]),
        ]
    return tuple(out)


def forward_slot(tables, gathered, floor, s):
    accs = tuple(jnp.zeros((8, LANES), F32) for _ in range(8))
    for j in range(WIDTH // LANES):
        degrees = s * WIDTH + j * LANES + lane_iota((8, LANES))
        accs = forward_column(accs, tables, gathered, s, s, j, degrees >= floor)

    def step(b, accs):
        for j in range(WIDTH // LANES):
            accs = forward_column(accs, tables, gathered, s, b, j)
        return accs

    return lax.fori_loop(s + 1, BLOCKS, step, accs)


def forward_kernel(ids_ref, leg_ref, gathered, out_ref, tables, sems):
    copies = table_copies(leg_ref, tables, sems)
    for copy in reversed(copies):
        copy.start()
    slot_of_lane = lane_iota((8, LANES)) % SLOTS
    sums = [jnp.zeros((8, LANES), F32) for _ in range(8)]
    orders = jnp.zeros((8, LANES), F32)
    for s in reversed(range(SLOTS)):
        here = slot_of_lane == s
        orders = jnp.where(here, ids_ref[s].astype(F32), orders)
        copies[s].wait()
        accs = forward_slot(tables, gathered, jnp.maximum(ids_ref[s], 2), s)
        for i in range(8):
            sums[i] = jnp.where(here, jnp.sum(accs[i], axis=1, keepdims=True), sums[i])
    zero = jnp.zeros((8, LANES), F32)
    for half in range(2):
        rows = sums[half * 4 : half * 4 + 4] + [orders, zero, zero, zero]
        for a in range(8):
            out_ref[pl.ds(half * 64 + a, 8, stride=8), :] = rows[a]


def forward(order_ids, legendre, gathered):
    return pl.pallas_call(
        forward_kernel,
        out_shape=jax.ShapeDtypeStruct((128, LANES), F32),
        in_specs=[
            pl.BlockSpec(memory_space=pltpu.SMEM),
            pl.BlockSpec(memory_space=pl.ANY),
            pl.BlockSpec(memory_space=pltpu.VMEM),
        ],
        out_specs=pl.BlockSpec(memory_space=pltpu.VMEM),
        scratch_shapes=[
            pltpu.VMEM(legendre.shape, F32),
            pltpu.SemaphoreType.DMA((SLOTS,)),
        ],
        compiler_params=pltpu.CompilerParams(vmem_limit_bytes=VMEM_LIMIT),
        name="forward",
    )(order_ids, legendre, gathered)


def turn_tables(n, quarter_rate, half_length, unit):
    turns = jnp.floor(n * quarter_rate + 0.5)
    x = (n - turns * half_length) * unit
    q = turns.astype(jnp.int32) & 3
    z = x * x
    sin = ((-1.9515295891e-4 * z + 8.3321608736e-3) * z - 1.6666654611e-1) * z * x + x
    cos = (
        (2.443315711809948e-5 * z - 1.388731625493765e-3) * z + 4.166664568298827e-2
    ) * z * z - 0.5 * z + 1.0
    odd = (q & 1) == 1
    c = jnp.where(odd, sin, cos)
    s = jnp.where(odd, cos, sin)
    c = jnp.where((q == 1) | (q == 2), -c, c)
    s = jnp.where(q >= 2, -s, s)
    return c, s


def wrap(n, period):
    rest = n - jnp.floor(n / period) * period
    rest = jnp.where(rest < 0.0, rest + period, rest)
    return jnp.where(rest >= period, rest - period, rest)


def cycle_setup(orders, length, offset):
    length_row = jnp.full((1, LANES), length.astype(F32))
    period = 2.0 * length_row
    half_length = 0.5 * length_row
    quarter_rate = 2.0 / length_row
    unit = math.pi / length_row
    low = wrap(orders, period)
    high = wrap(low * 256.0, period)
    shape = (256, LANES)
    kh = (row_iota(shape) // 2).astype(F32)
    kl = (2 * row_iota((LANES, LANES)) + offset).astype(F32)
    cos_a, sin_a = turn_tables(high * kh, quarter_rate, half_length, unit)
    cos_b, sin_b = turn_tables(low * kl, quarter_rate, half_length, unit)
    return cos_a, sin_a, jnp.concatenate([cos_b, sin_b], axis=1)


def cycle_phase(block, sky, length, offset, weight):
    orders = block[4:5, :]
    cos_a, sin_a, table = cycle_setup(orders, length, offset)
    factor = jnp.where(orders == 0.0, 1.0, 2.0)
    scaled = block * factor
    shape = (256, LANES)
    rows = row_iota(shape)
    first = (rows & 1) == 0
    real = jnp.where(first, scaled[0:1, :], scaled[2:3, :])
    imag = jnp.where(first, scaled[1:2, :], scaled[3:4, :])
    left = jnp.concatenate(
        [real * cos_a - imag * sin_a, -(real * sin_a + imag * cos_a)], axis=1
    )
    model = lax.dot_general(
        left, table, (((1,), (1,)), ((), ())), precision=HIGHEST, preferred_element_type=F32
    )
    pixels = (rows // 2) * LANES + lane_iota(shape)
    residual = jnp.where(pixels < length, sky - model, 0.0)
    totals = lax.dot_general(
        residual, table, (((1,), (0,)), ((), ())), precision=HIGHEST, preferred_element_type=F32
    )
    tc, ts = totals[:, :LANES], totals[:, LANES:]
    cos_sum = jnp.sum((cos_a * tc - sin_a * ts).reshape(32, 8, LANES), axis=0)
    sin_sum = jnp.sum((sin_a * tc + cos_a * ts).reshape(32, 8, LANES), axis=0)
    out = []
    for part in (cos_sum, sin_sum):
        part = part + pltpu.roll(part, 2, 0)
        out.append(part + pltpu.roll(part, 4, 0))
    cos_sum, sin_sum = out
    rows = row_iota((8, LANES))
    analysed = jnp.where(
        rows == 0,
        cos_sum[0:1, :],
        jnp.where(
            rows == 1,
            -sin_sum[0:1, :],
            jnp.where(rows == 2, cos_sum[1:2, :], jnp.where(rows == 3, -sin_sum[1:2, :], 0.0)),
        ),
    )
    return residual, analysed * weight


def pixel_kernel(scale, length, offset, weight, phases, sky, residual_ref, out_ref):
    owner = lane_iota((8, LANES)) // SLOTS
    for c in range(2):
        block = jnp.zeros((8, LANES), F32)
        for o in range(GROUP):
            piece = phases[o * 16 + c * 8 : o * 16 + c * 8 + 8, :]
            block = jnp.where(owner == o, piece, block)
        residual, analysed = cycle_phase(
            block, sky[c], length[c], offset[c], weight[c] * scale
        )
        residual_ref[c] = residual
        for o in range(GROUP):
            out_ref[o * 16 + c * 8 : o * 16 + c * 8 + 8, :] = analysed


def pixel_phase(scale, length, offset, weight, phases, sky):
    smem = pl.BlockSpec(memory_space=pltpu.SMEM)
    vmem = pl.BlockSpec(memory_space=pltpu.VMEM)
    return pl.pallas_call(
        functools.partial(pixel_kernel, scale),
        out_shape=(
            jax.ShapeDtypeStruct(sky.shape, F32),
            jax.ShapeDtypeStruct((128, LANES), F32),
        ),
        in_specs=[smem, smem, smem, vmem, vmem],
        out_specs=(vmem, vmem),
        name="pixel_phase",
    )(length, offset, weight, phases, sky)


def merge_rows(x, y, shift, bit):
    return jnp.where(bit, y, x) + pltpu.roll(jnp.where(bit, x, y), shift, 0)


def adjoint_tile(tables, weights, s, b, store):
    rows = row_iota((8, LANES))
    bits = [(rows & n) != 0 for n in (1, 2, 4)]
    for pair in range(WIDTH // LANES // 2):
        parts = []
        for j in (2 * pair, 2 * pair + 1):
            lanes = pl.ds(pl.multiple_of(b * WIDTH + j * LANES, LANES), LANES)
            sums = [None] * 4
            for half in range(2):
                plus = tables[s, 0, half * 8 : half * 8 + 8, lanes]
                minus = tables[s, 1, half * 8 : half * 8 + 8, lanes]
                w = weights[half * 4 : half * 4 + 4]
                terms = [
                    minus * w[3] - plus * w[0],
                    -(plus * w[1] + minus * w[2]),
                    -(plus * w[2] + minus * w[1]),
                    minus * w[0] - plus * w[3],
                ]
                sums = [t if x is None else x + t for x, t in zip(sums, terms)]
            parts += sums
        for level, shift in enumerate((1, 2, 4)):
            parts = [
                merge_rows(parts[2 * i], parts[2 * i + 1], shift, bits[level])
                for i in range(len(parts) // 2)
            ]
        store(pair, parts[0])


def slot_weights(columns, s):
    return [jnp.broadcast_to(c[:, s : s + 1], (8, LANES)) for c in columns]


def own_columns(returned, me):
    columns = []
    shift = (LANES - SLOTS * me) % LANES
    for half in range(2):
        for a in range(4):
            rows = returned[pl.ds(half * 64 + a, 8, stride=8), :]
            columns.append(pltpu.roll(rows, shift, 1))
    return columns


def adjoint_kernel(leg_ref, returned, out_ref, tables, sems):
    copies = table_copies(leg_ref, tables, sems)
    for copy in reversed(copies):
        copy.start()
    columns = own_columns(returned, lax.axis_index("order"))
    for s in reversed(range(SLOTS)):
        weights = slot_weights(columns, s)
        copies[s].wait()

        def clear(b, carry):
            out_ref[b, s] = jnp.zeros((4, WIDTH), F32)
            return carry

        def step(b, carry):
            def store(pair, block):
                out_ref[b, s, :, pair * 256 : pair * 256 + 128] = block[0:4]
                out_ref[b, s, :, pair * 256 + 128 : pair * 256 + 256] = block[4:8]

            adjoint_tile(tables, weights, s, b, store)
            return carry

        lax.fori_loop(0, s, clear, 0)
        lax.fori_loop(s, BLOCKS, step, 0)


def adjoint(legendre, returned):
    return pl.pallas_call(
        adjoint_kernel,
        out_shape=jax.ShapeDtypeStruct((BLOCKS, SLOTS, 4, WIDTH), F32),
        in_specs=[
            pl.BlockSpec(memory_space=pl.ANY),
            pl.BlockSpec(memory_space=pltpu.VMEM),
        ],
        out_specs=pl.BlockSpec(memory_space=pltpu.VMEM),
        scratch_shapes=[
            pltpu.VMEM(legendre.shape, F32),
            pltpu.SemaphoreType.DMA((SLOTS,)),
        ],
        compiler_params=pltpu.CompilerParams(vmem_limit_bytes=VMEM_LIMIT),
        name="adjoint",
    )(legendre, returned)


def to_rows(sky):
    cycles = sky.shape[0]
    parts = sky.reshape(cycles, 2, LANES, LANES)
    return jnp.transpose(parts, (0, 2, 1, 3)).reshape(cycles, 2 * LANES, LANES)


def from_rows(rows):
    cycles = rows.shape[0]
    parts = rows.reshape(cycles, LANES, 2, LANES)
    return jnp.transpose(parts, (0, 2, 1, 3)).reshape(cycles, 2, LANES * LANES)


def body(harmonics, legendre, sky_map, cycle_length, cycle_offset, cycle_weight, order_ids):
    scale = math.sqrt(8192 * 128 / 4194304)
    gathered = lax.all_gather(harmonics, "blk", axis=0)
    message = forward(order_ids, legendre, gathered)
    phases = lax.all_to_all(
        message.reshape(GROUP, 16, LANES), "order", split_axis=0, concat_axis=0
    ).reshape(128, LANES)
    rows, message = pixel_phase(
        scale, cycle_length, cycle_offset, cycle_weight, phases, to_rows(sky_map)
    )
    returned = lax.all_to_all(
        message.reshape(GROUP, 16, LANES), "order", split_axis=0, concat_axis=0
    ).reshape(128, LANES)
    update = adjoint(legendre, returned)
    own_update = lax.psum_scatter(update, "blk", scatter_dimension=0)
    degrees = lax.axis_index("blk") * WIDTH + lax.iota(jnp.int32, WIDTH)
    floors = jnp.maximum(order_ids, 2)
    mask = (degrees[None, :] >= floors[:, None])[:, None, :]
    refined = jnp.where(mask, harmonics + own_update, 0.0)
    return refined, from_rows(rows)


def solution(mesh):
    return jax.shard_map(
        body,
        mesh=mesh,
        in_specs=(
            P("order", None, "blk"),
            P("order", None, "blk", None),
            P(("blk", "order"), None, None),
            P(("blk", "order")),
            P(("blk", "order")),
            P(("blk", "order")),
            P("order"),
        ),
        out_specs=(P("order", None, "blk"), P(("blk", "order"), None, None)),
        check_vma=False,
    )
```

time: 620 us -> 183 us (0.30)
  other arithmetic: 243 us -> 1.05 us
  matrix products: 119 us -> 0 us
  local copies, waits for them, and re-layouts: 93.5 us -> 4.93 us
  Pallas kernels: 0 us -> 20.6 us
    cos x16 -> x0, other arithmetic: 221 us -> none  [cycle_tables(): return (jnp.concatenate([jnp.cos(angles), jnp.sin(angles)], axis=0), inside)]
    dot_general x34 -> x0, matrix products: 119 us -> none  [the longest x1 61.1 us: body(): jnp.einsum('mtrl,mcl->mtcr', legendre, section * keep_mask[:, None, :], p...]
    unnamed x28 -> x5, local copies, waits for them, and re-layouts: 88.6 us -> 1.36 us
    pallas_call x0 -> x3, Pallas kernels: none -> 20.6 us  [the longest x1 8.93 us: adjoint(): pl.pallas_call(adjoint_kernel, out_shape=jax.ShapeDtypeStruct((BLOCKS, SL...]
    all_to_all x1 -> x2, blocking collectives: 7.65 us -> 19.6 us  [body(): lax.all_to_all(message.reshape(GROUP, 16, LANES), 'order', split_axis=0,...]
    all_gather x1, waiting for transfers between devices: 38.9 us -> 49.7 us  [body(): gathered = lax.all_gather(harmonics, 'blk', axis=0)]
    convert_element_type x18 -> x0, other arithmetic: 10.5 us -> none  [the longest x16 10.3 us: cycle_tables(): inside = (pixels < length).astype(jnp.float32)]
    add x18 -> x1, other arithmetic: 9.38 us -> 0.01 us  [body(): degrees = lax.axis_index('blk') * WIDTH + lax.iota(jnp.int32, WIDTH)]
  transfers between devices with their start and end apart: 3 -> 2, of which waited for: 3 -> 2; matrix products, arithmetic and copies ran while one was open for 0% -> 0% of each run, Pallas kernels for 0% -> 0%
where the time goes in v1:
time: 183 us
  waiting for transfers between devices  123 us (67%)
  Pallas kernels  20.6 us (11%)
  blocking collectives  19.6 us (11%)
  between operations  14.1 us (8%)
  local copies, waits for them, and re-layouts  4.93 us (3%)
    unnamed x3, waiting for transfers between devices  72.9 us
    all_gather x1, waiting for transfers between devices, body(): gathered = lax.all_gather(harmonics, 'blk', axis=0)  49.7 us
    all_to_all x2, blocking collectives, body(): lax.all_to_all(message.reshape(GROUP, 16, LANES), 'order', split_axis=0,...  19.6 us
    pallas_call x1, Pallas kernels, adjoint(): pl.pallas_call(adjoint_kernel, out_shape=jax.ShapeDtypeStruct((BLOCKS, SL...  8.93 us
    pallas_call x1, Pallas kernels, forward(): pl.pallas_call(forward_kernel, out_shape=jax.ShapeDtypeStruct((128, LANES...  7.61 us
    pallas_call x1, Pallas kernels, pixel_phase(): pl.pallas_call(functools.partial(pixel_kernel, scale), out_shape=(jax.Sha...  4.04 us
  transfers between devices with their start and end apart: 2, of which 2 were waited for; matrix products, arithmetic and copies ran while one was open for 0% of the time, Pallas kernels for 0%

profile of v1, /device:TPU:0, one launch (start us, length us, event | category | flops | bytes accessed | tf_op | source)
XLA Modules:
  0.0 182.9 jit_solution(13520372338616063475)
XLA Ops:
  7.2 0.0 all-gather.3.cloned.1.call-start
  7.2 0.7 all-gather.3.cloned.1.call-update
  7.9 0.0 reduce-scatter.4.cloned.1.call-start
  7.9 49.7 %all-gather.3.cloned.1.call-done = f32[256,4,512]{2,1,0:T(4,128)} async-done(((f32[16,4,512]{2,1,0:T(4,128)}), f32[256,4,512]{2,1,0:T(4,128)}) %all-gather.3.cloned.1.call-update) | async-done | bytes 2097168 | tf_op jit(solution)/shard_map/all_gather | solution.py:331
  57.7 7.6 %forward.1 = f32[128,128]{1,0:T(8,128)} custom-call(s32[16]{0:T(128)} %ids_ref.1, f32[16,2,16,8192]{3,2,1,0:T(8,128)} %leg_ref.3, f32[16,16,4,512]{3,2,1,0:T(4,128)} %bitcast.20), custom_call_target="tpu_custom_call" | custom-call | tf_op jit(solution)/shard_map/forward/pallas_call | solution.py:99
  65.3 10.0 %all_to_all.10 = f32[8,16,128]{2,1,0:T(8,128)} all-to-all(f32[8,16,128]{2,1,0:T(8,128)} %bitcast.21), channel_id=1, replica_groups=mesh['blk'=16,'order'=8] {'order'}, dimensions={0} | all-to-all | bytes 131072 | tf_op jit(solution)/shard_map/all_to_all | solution.py:333
  75.3 4.0 %pixel_phase.1 = (f32[2,256,128]{2,1,0:T(8,128)}, f32[128,128]{1,0:T(8,128)}) custom-call(s32[2]{0:T(128)} %length.1, s32[2]{0:T(128)} %offset.1, f32[2]{0:T(128)} %weight.1, f32[128,128]{1,0:T(8,128)} %bitcast.24, f32[2,256,128]{2,1,0:T(8,128)} %bitcast.23), custom_call_target="tpu_custom_call" | custom-call | tf_op jit(solution)/shard_map/pixel_phase/pallas_call | solution.py:216
  79.3 9.6 %all_to_all.11 = f32[8,16,128]{2,1,0:T(8,128)} all-to-all(f32[8,16,128]{2,1,0:T(8,128)} %bitcast.25), channel_id=1, replica_groups=mesh['blk'=16,'order'=8] {'order'}, dimensions={0} | all-to-all | bytes 131072 | tf_op jit(solution)/shard_map/all_to_all | solution.py:339
  88.9 8.9 %adjoint.1 = f32[16,16,4,512]{3,2,1,0:T(4,128)} custom-call(f32[16,2,16,8192]{3,2,1,0:T(8,128)} %leg_ref.3, f32[128,128]{1,0:T(8,128)} %bitcast.22), custom_call_target="tpu_custom_call" | custom-call | tf_op jit(solution)/shard_map/adjoint/pallas_call | solution.py:300
  97.8 3.6 %copy.12 = f32[16,16,4,512]{3,1,2,0:T(8,128)} copy(f32[16,16,4,512]{3,2,1,0:T(4,128)} %adjoint.1) | data formatting | bytes 4194304 | tf_op jit(solution)/shard_map/adjoint/pallas_call | solution.py:300
  101.4 0.0 copy-start.1
  101.4 0.0 copy-start
  101.4 0.0 reduce-scatter.4.cloned.1.call-update
  101.4 0.6 copy-done.1
  102.1 0.1 broadcast_compare_fusion
  102.1 72.2 %reduce-scatter.4.cloned.1.call-done = f32[1,16,4,512]{3,1,2,0:T(8,128)} async-done(((f32[16,16,4,512]{3,1,2,0:T(8,128)}), f32[1,16,4,512]{3,1,2,0:T(8,128)}) %reduce-scatter.4.cloned.1.call-update) | async-done | bytes 131088
  174.3 0.0 copy-done
  174.3 1.0 fusion
  175.3 0.7 copy.15
  (2 shorter events, 0.0 us)
Async XLA Ops:
  7.2 50.5 %all-gather.3.cloned.1.call-start = ((), (), s32[]{:S(2)}) async-start(), calls=%async_computation.3 | async-start | bytes 2228224 | tf_op jit(solution)/shard_map/all_gather | solution.py:331
  7.9 166.4 %reduce-scatter.4.cloned.1.call-start = ((), (), s32[]{:S(2)}) async-start(), calls=%async_computation.4 | async-start | bytes 2228224
  101.4 0.7 copy-start.1
  101.4 72.9 %copy-start = (f32[16,4,512]{2,1,0:T(4,128)S(1)}, f32[16,4,512]{2,1,0:T(4,128)}, u32[]{:S(2)}) copy-start(f32[16,4,512]{2,1,0:T(4,128)} %param.7) | copy-start | bytes 393220
Sparse Core Ops, SparseCore 0:
  10.1 47.5 all-gather.2
  101.6 72.7 reduce-scatter.3

commit v2 on v1

v2 whole, which is shorter than its diff:
```python
import functools
import math

import jax
import jax.numpy as jnp
from jax import lax
from jax.experimental import pallas as pl
from jax.experimental.pallas import tpu as pltpu
from jax.sharding import PartitionSpec as P

HIGHEST = lax.Precision.HIGHEST
F32 = jnp.float32
SLOTS = 16
BLOCKS = 16
WIDTH = 512
GROUP = 8
LANES = 128
HALF = WIDTH // 2
VMEM_LIMIT = 60 * 1024 * 1024


def lane_iota(shape):
    return lax.broadcasted_iota(jnp.int32, shape, len(shape) - 1)


def row_iota(shape):
    return lax.broadcasted_iota(jnp.int32, shape, 0)


def slot_pairs(b):
    return (b + 2) // 2


def table_copies(leg_ref, tables, sems):
    copies = []
    for s in range(SLOTS):
        cut = pl.ds(s // 2 * 2 * WIDTH, (BLOCKS - s // 2 * 2) * WIDTH)
        copies.append(
            pltpu.make_async_copy(
                leg_ref.at[s, :, :, cut], tables.at[s, :, :, cut], sems.at[s]
            )
        )
    return copies


LEGS = [(0, 0, d, relay) for relay in (0, 1) for d in (1, -1)]
LEGS += [(1, f, d, relay) for f in (0, 1, -1, 2) for relay in (0, 1) for d in (1, -1)]
LEG_INDEX = {leg: k for k, leg in enumerate(LEGS)}


class Routes:
    def __init__(self):
        blk = lax.axis_index("blk")
        self.y, self.z = blk // 4, blk % 4
        self.me = blk

    def block(self, h, f, s):
        dy, dz = (f, s) if h == 0 else (s, f)
        return (self.y + dy + 8) % 4 * 4 + (self.z + dz + 8) % 4

    def neighbour(self, h, leg, sign):
        axis, _, d, _ = leg
        return self.block(h, sign * d, 0) if axis == 0 else self.block(h, 0, sign * d)

    def sent(self, h, leg):
        axis, f, d, relay = leg
        back = -d if relay else 0
        return self.block(h, back, 0) if axis == 0 else self.block(h, f, back)

    def received(self, h, leg):
        axis, f, d, relay = leg
        back = -2 * d if relay else -d
        return self.block(h, back, 0) if axis == 0 else self.block(h, f, back)

    def neighbours(self):
        return [self.block(0, 1, 0), self.block(0, -1, 0), self.block(0, 0, 1), self.block(0, 0, -1)]


CUTS = 4


def leg_cuts(b):
    return b // 4 + 1


def leg_cut(leg, b, c):
    _, _, d, relay = leg
    size = 2 if relay else 4
    first = 2 * leg_cuts(b) if relay and d == -1 else 0
    return pl.ds(first + c * size, size)


def each_cut(b, act):
    def step(c, carry):
        act(c)
        return carry

    lax.fori_loop(0, leg_cuts(b), step, 0)


def greet(axis, partners):
    barrier = pltpu.get_barrier_semaphore()
    for partner in partners:
        pl.semaphore_signal(barrier, 1, device_id={axis: partner})
    pl.semaphore_wait(barrier, len(partners))


def forward_pair(acc, tables, gathered, ids_ref, b, i, masked):
    for s in (2 * i, 2 * i + 1):
        accs = [acc[s, q] for q in range(8)]
        for j in range(WIDTH // LANES):
            lanes = pl.ds(pl.multiple_of(b * WIDTH + j * LANES, LANES), LANES)
            h, at = j // 2, j % 2 * LANES
            values = [
                jnp.broadcast_to(gathered[h, b, s, a : a + 1, at : at + LANES], (8, LANES))
                for a in range(4)
            ]
            if masked:
                degrees = b * WIDTH + j * LANES + lane_iota((8, LANES))
                keep = degrees >= jnp.maximum(ids_ref[s], 2)
                values = [jnp.where(keep, v, 0.0) for v in values]
            for r in range(2):
                plus = tables[s, 0, r * 8 : r * 8 + 8, lanes]
                minus = tables[s, 1, r * 8 : r * 8 + 8, lanes]
                a0, a1, a2, a3 = accs[r * 4 : r * 4 + 4]
                accs[r * 4 : r * 4 + 4] = [
                    a0 + (minus * values[3] - plus * values[0]),
                    a1 - (plus * values[1] + minus * values[2]),
                    a2 - (plus * values[2] + minus * values[1]),
                    a3 + (minus * values[0] - plus * values[3]),
                ]
        for q in range(8):
            acc[s, q] = accs[q]


def forward_block(acc, tables, gathered, ids_ref, b):
    last = slot_pairs(b) - 1

    def step(i, carry):
        forward_pair(acc, tables, gathered, ids_ref, b, i, False)
        return carry

    lax.fori_loop(0, last, step, 0)
    forward_pair(acc, tables, gathered, ids_ref, b, last, True)


def write_message(acc, ids_ref, out_ref):
    slot_of_lane = lane_iota((8, LANES)) % SLOTS
    sums = [jnp.zeros((8, LANES), F32) for _ in range(8)]
    orders = jnp.zeros((8, LANES), F32)
    for s in range(SLOTS):
        here = slot_of_lane == s
        orders = jnp.where(here, ids_ref[s].astype(F32), orders)
        for q in range(8):
            sums[q] = jnp.where(here, jnp.sum(acc[s, q], axis=1, keepdims=True), sums[q])
    zero = jnp.zeros((8, LANES), F32)
    for r in range(2):
        rows = sums[r * 4 : r * 4 + 4] + [orders, zero, zero, zero]
        for a in range(8):
            for i in range(8):
                at = r * 64 + i * 8 + a
                out_ref[at : at + 1, :] = rows[a][i : i + 1, :]


def gather_forward_kernel(
    ids_ref, leg_ref, harm_ref, out_ref, tables, gathered, acc,
    table_sems, own_sems, send_sems, recv_sems,
):
    routes = Routes()
    loads = table_copies(leg_ref, tables, table_sems)
    own = [
        pltpu.make_async_copy(
            harm_ref.at[:, :, pl.ds(h * HALF, HALF)], gathered.at[h, routes.me], own_sems.at[h]
        )
        for h in range(2)
    ]
    greet("blk", routes.neighbours())

    def copy(h, leg, b, target, c):
        cut = leg_cut(leg, b, c)
        k = (h * len(LEGS) + LEG_INDEX[leg]) * CUTS + c
        axis, f, d, relay = leg
        source = gathered.at[h, b, cut]
        if f == 0 and not relay:
            source = harm_ref.at[cut, :, pl.ds(h * HALF, HALF)]
        return pltpu.make_async_remote_copy(
            src_ref=source,
            dst_ref=gathered.at[h, b, cut],
            send_sem=send_sems.at[k],
            recv_sem=recv_sems.at[k],
            device_id={"blk": target},
        )

    started = []

    def send(*leg):
        for h in range(2):
            for d in (1, -1):
                full = (leg[0], leg[1], d, leg[2])
                b, target = routes.sent(h, full), routes.neighbour(h, full, 1)
                each_cut(b, lambda c: copy(h, full, b, target, c).start())
                started.append((h, full, b, target))

    def arrive(*leg):
        for h in range(2):
            for d in (1, -1):
                full = (leg[0], leg[1], d, leg[2])
                b, target = routes.received(h, full), routes.neighbour(h, full, 1)
                each_cut(b, lambda c: copy(h, full, b, target, c).wait_recv())

    def compute(places):
        for dy, dz in places:
            forward_block(acc, tables, gathered, ids_ref, routes.block(0, dy, dz))

    send(0, 0, 0)
    send(1, 0, 0)
    for c in own + loads[::-1]:
        c.start()
    for s in range(SLOTS):
        for q in range(8):
            acc[s, q] = jnp.zeros((8, LANES), F32)
    arrive(0, 0, 0)
    send(1, 1, 0)
    send(1, -1, 0)
    send(0, 0, 1)
    arrive(1, 0, 0)
    send(1, 0, 1)
    for c in own + loads[::-1]:
        c.wait()
    compute([(0, 0), (1, 0), (-1, 0)])
    arrive(0, 0, 1)
    send(1, 2, 0)
    arrive(1, 1, 0)
    send(1, 1, 1)
    arrive(1, -1, 0)
    send(1, -1, 1)
    arrive(1, 0, 1)
    compute([(0, 1), (0, -1), (1, 1), (1, -1), (-1, 1), (-1, -1)])
    arrive(1, 2, 0)
    send(1, 2, 1)
    compute([(2, 0), (0, 2)])
    arrive(1, 1, 1)
    arrive(1, -1, 1)
    compute([(2, 1), (2, -1), (1, 2), (-1, 2)])
    arrive(1, 2, 1)
    compute([(2, 2)])
    write_message(acc, ids_ref, out_ref)
    for h, full, b, target in started:
        each_cut(b, lambda c: copy(h, full, b, target, c).wait_send())


def gather_forward(order_ids, legendre, harmonics):
    legs = 2 * len(LEGS)
    return pl.pallas_call(
        gather_forward_kernel,
        out_shape=jax.ShapeDtypeStruct((128, LANES), F32),
        in_specs=[
            pl.BlockSpec(memory_space=pltpu.SMEM),
            pl.BlockSpec(memory_space=pl.ANY),
            pl.BlockSpec(memory_space=pl.ANY),
        ],
        out_specs=pl.BlockSpec(memory_space=pltpu.VMEM),
        scratch_shapes=[
            pltpu.VMEM(legendre.shape, F32),
            pltpu.VMEM((2, BLOCKS, SLOTS, 4, HALF), F32),
            pltpu.VMEM((SLOTS, 8, 8, LANES), F32),
            pltpu.SemaphoreType.DMA((SLOTS,)),
            pltpu.SemaphoreType.DMA((2,)),
            pltpu.SemaphoreType.DMA((legs * CUTS,)),
            pltpu.SemaphoreType.DMA((legs * CUTS,)),
        ],
        compiler_params=pltpu.CompilerParams(
            collective_id=0, has_side_effects=True, vmem_limit_bytes=VMEM_LIMIT
        ),
        name="gather_forward",
    )(order_ids, legendre, harmonics)


def turn_tables(n, quarter_rate, half_length, unit):
    turns = jnp.floor(n * quarter_rate + 0.5)
    x = (n - turns * half_length) * unit
    q = turns.astype(jnp.int32) & 3
    z = x * x
    sin = ((-1.9515295891e-4 * z + 8.3321608736e-3) * z - 1.6666654611e-1) * z * x + x
    cos = (
        (2.443315711809948e-5 * z - 1.388731625493765e-3) * z + 4.166664568298827e-2
    ) * z * z - 0.5 * z + 1.0
    odd = (q & 1) == 1
    c = jnp.where(odd, sin, cos)
    s = jnp.where(odd, cos, sin)
    c = jnp.where((q == 1) | (q == 2), -c, c)
    s = jnp.where(q >= 2, -s, s)
    return c, s


def wrap(n, period):
    rest = n - jnp.floor(n / period) * period
    rest = jnp.where(rest < 0.0, rest + period, rest)
    return jnp.where(rest >= period, rest - period, rest)


def cycle_setup(orders, length, offset):
    length_row = jnp.full((1, LANES), length.astype(F32))
    period = 2.0 * length_row
    half_length = 0.5 * length_row
    quarter_rate = 2.0 / length_row
    unit = math.pi / length_row
    low = wrap(orders, period)
    high = wrap(low * 256.0, period)
    shape = (256, LANES)
    kh = (row_iota(shape) // 2).astype(F32)
    kl = (2 * row_iota((LANES, LANES)) + offset).astype(F32)
    cos_a, sin_a = turn_tables(high * kh, quarter_rate, half_length, unit)
    cos_b, sin_b = turn_tables(low * kl, quarter_rate, half_length, unit)
    return cos_a, sin_a, jnp.concatenate([cos_b, sin_b], axis=1)


def cycle_phase(block, sky, length, offset, weight):
    orders = block[4:5, :]
    cos_a, sin_a, table = cycle_setup(orders, length, offset)
    factor = jnp.where(orders == 0.0, 1.0, 2.0)
    scaled = block * factor
    shape = (256, LANES)
    rows = row_iota(shape)
    first = (rows & 1) == 0
    real = jnp.where(first, scaled[0:1, :], scaled[2:3, :])
    imag = jnp.where(first, scaled[1:2, :], scaled[3:4, :])
    left = jnp.concatenate(
        [real * cos_a - imag * sin_a, -(real * sin_a + imag * cos_a)], axis=1
    )
    model = lax.dot_general(
        left, table, (((1,), (1,)), ((), ())), precision=HIGHEST, preferred_element_type=F32
    )
    pixels = (rows // 2) * LANES + lane_iota(shape)
    residual = jnp.where(pixels < length, sky - model, 0.0)
    totals = lax.dot_general(
        residual, table, (((1,), (0,)), ((), ())), precision=HIGHEST, preferred_element_type=F32
    )
    tc, ts = totals[:, :LANES], totals[:, LANES:]
    cos_sum = jnp.sum((cos_a * tc - sin_a * ts).reshape(32, 8, LANES), axis=0)
    sin_sum = jnp.sum((sin_a * tc + cos_a * ts).reshape(32, 8, LANES), axis=0)
    out = []
    for part in (cos_sum, sin_sum):
        part = part + pltpu.roll(part, 2, 0)
        out.append(part + pltpu.roll(part, 4, 0))
    cos_sum, sin_sum = out
    rows = row_iota((8, LANES))
    analysed = jnp.where(
        rows == 0,
        cos_sum[0:1, :],
        jnp.where(
            rows == 1,
            -sin_sum[0:1, :],
            jnp.where(rows == 2, cos_sum[1:2, :], jnp.where(rows == 3, -sin_sum[1:2, :], 0.0)),
        ),
    )
    return residual, analysed * weight


def pixel_kernel(
    scale, length, offset, weight, message, sky, residual_ref, returned,
    phases, reply, send_sems, recv_sems,
):
    me = lax.axis_index("order")
    greet("order", [(me + d) % GROUP for d in range(1, GROUP)])

    def rows_of(o):
        return pl.ds(pl.multiple_of(o * 16, 16), 16)

    def copies(way, source, target):
        out = []
        for d in range(1, GROUP):
            k = way * GROUP + d
            out.append(
                pltpu.make_async_remote_copy(
                    src_ref=source((me + d) % GROUP),
                    dst_ref=target.at[rows_of(me)],
                    send_sem=send_sems.at[k],
                    recv_sem=recv_sems.at[k],
                    device_id={"order": (me + d) % GROUP},
                )
            )
        return out

    out = copies(0, lambda o: message.at[rows_of(o)], phases)
    for c in out:
        c.start()
    phases[rows_of(me), :] = message[rows_of(me), :]
    for c in out:
        c.wait_recv()
    owner = lane_iota((8, LANES)) // SLOTS
    for c in range(2):
        block = jnp.zeros((8, LANES), F32)
        for o in range(GROUP):
            piece = phases[o * 16 + c * 8 : o * 16 + c * 8 + 8, :]
            block = jnp.where(owner == o, piece, block)
        residual, analysed = cycle_phase(
            block, sky[c], length[c], offset[c], weight[c] * scale
        )
        residual_ref[c] = residual
        reply[c * 8 : c * 8 + 8, :] = analysed
    back = copies(1, lambda o: reply, returned)
    for c in back:
        c.start()
    returned[rows_of(me), :] = reply[...]
    for c in back:
        c.wait_recv()
    for c in out + back:
        c.wait_send()


def pixel_phase(scale, length, offset, weight, message, sky):
    smem = pl.BlockSpec(memory_space=pltpu.SMEM)
    vmem = pl.BlockSpec(memory_space=pltpu.VMEM)
    return pl.pallas_call(
        functools.partial(pixel_kernel, scale),
        out_shape=(
            jax.ShapeDtypeStruct(sky.shape, F32),
            jax.ShapeDtypeStruct((128, LANES), F32),
        ),
        in_specs=[smem, smem, smem, vmem, vmem],
        out_specs=(vmem, vmem),
        scratch_shapes=[
            pltpu.VMEM((128, LANES), F32),
            pltpu.VMEM((16, LANES), F32),
            pltpu.SemaphoreType.DMA((2 * GROUP,)),
            pltpu.SemaphoreType.DMA((2 * GROUP,)),
        ],
        compiler_params=pltpu.CompilerParams(collective_id=1, has_side_effects=True),
        name="pixel_phase",
    )(length, offset, weight, message, sky)


def merge_rows(x, y, shift, bit):
    return jnp.where(bit, y, x) + pltpu.roll(jnp.where(bit, x, y), shift, 0)


def adjoint_pair(update, tables, weights, bits, b, i):
    for s in (2 * i, 2 * i + 1):
        w = [weights[s, q] for q in range(8)]
        for h in range(2):
            parts = []
            for j in (2 * h, 2 * h + 1):
                lanes = pl.ds(pl.multiple_of(b * WIDTH + j * LANES, LANES), LANES)
                sums = [None] * 4
                for r in range(2):
                    plus = tables[s, 0, r * 8 : r * 8 + 8, lanes]
                    minus = tables[s, 1, r * 8 : r * 8 + 8, lanes]
                    w0, w1, w2, w3 = w[r * 4 : r * 4 + 4]
                    terms = [
                        minus * w3 - plus * w0,
                        -(plus * w1 + minus * w2),
                        -(plus * w2 + minus * w1),
                        minus * w0 - plus * w3,
                    ]
                    sums = [t if x is None else x + t for x, t in zip(sums, terms)]
                parts += sums
            for level, shift in enumerate((1, 2, 4)):
                parts = [
                    merge_rows(parts[2 * n], parts[2 * n + 1], shift, bits[level])
                    for n in range(len(parts) // 2)
                ]
            update[h, b, s, :, 0:LANES] = parts[0][0:4]
            update[h, b, s, :, LANES : 2 * LANES] = parts[0][4:8]


def adjoint_block(update, tables, weights, b):
    rows = row_iota((8, LANES))
    bits = [(rows & n) != 0 for n in (1, 2, 4)]

    def step(i, carry):
        adjoint_pair(update, tables, weights, bits, b, i)
        return carry

    lax.fori_loop(0, slot_pairs(b), step, 0)


def write_weights(returned, weights, me):
    shift = (LANES - SLOTS * me) % LANES
    for r in range(2):
        for a in range(4):
            lines = [r * 64 + i * 8 + a for i in range(8)]
            rows = jnp.concatenate([returned[n : n + 1, :] for n in lines], axis=0)
            rows = pltpu.roll(rows, shift, 1)
            for s in range(SLOTS):
                weights[s, r * 4 + a] = jnp.broadcast_to(rows[:, s : s + 1], (8, LANES))


def adjoint_scatter_kernel(
    ids_ref, leg_ref, harm_ref, returned, refined, tables, update, landed, weights,
    table_sems, send_sems, recv_sems,
):
    routes = Routes()
    loads = table_copies(leg_ref, tables, table_sems)
    for c in loads[::-1]:
        c.start()
    greet("blk", routes.neighbours())
    write_weights(returned, weights, lax.axis_index("order"))
    for c in loads[::-1]:
        c.wait()

    def copy(h, leg, b, target, c):
        cut = leg_cut(leg, b, c)
        leg_id = h * len(LEGS) + LEG_INDEX[leg]
        k = leg_id * CUTS + c
        return pltpu.make_async_remote_copy(
            src_ref=update.at[h, b, cut],
            dst_ref=landed.at[leg_id, cut],
            send_sem=send_sems.at[k],
            recv_sem=recv_sems.at[k],
            device_id={"blk": target},
        )

    started = []

    def send(*leg):
        for h in range(2):
            for d in (1, -1):
                full = (leg[0], leg[1], d, leg[2])
                b, target = routes.received(h, full), routes.neighbour(h, full, -1)
                each_cut(b, lambda c: copy(h, full, b, target, c).start())
                started.append((h, full, b, target))

    def absorb(*leg):
        for h in range(2):
            for d in (1, -1):
                full = (leg[0], leg[1], d, leg[2])
                b, target = routes.sent(h, full), routes.neighbour(h, full, -1)
                k = h * len(LEGS) + LEG_INDEX[full]

                def add(c):
                    copy(h, full, b, target, c).wait_recv()
                    cut = leg_cut(full, b, c)
                    update[h, b, cut] = update[h, b, cut] + landed[k, cut]

                each_cut(b, add)

    def compute(places):
        for dy, dz in places:
            adjoint_block(update, tables, weights, routes.block(0, dy, dz))

    compute([(2, 2)])
    send(1, 2, 1)
    compute([(1, 2), (-1, 2), (2, 1), (2, -1)])
    send(1, 1, 1)
    send(1, -1, 1)
    absorb(1, 2, 1)
    send(1, 2, 0)
    compute([(2, 0), (0, 2)])
    send(1, 0, 1)
    compute([(1, 1), (1, -1), (-1, 1), (-1, -1)])
    absorb(1, 1, 1)
    absorb(1, -1, 1)
    send(1, 1, 0)
    send(1, -1, 0)
    absorb(1, 2, 0)
    send(0, 0, 1)
    compute([(1, 0), (-1, 0), (0, 1), (0, -1)])
    absorb(1, 0, 1)
    send(1, 0, 0)
    absorb(1, 1, 0)
    absorb(1, -1, 0)
    absorb(0, 0, 1)
    send(0, 0, 0)
    compute([(0, 0)])
    absorb(1, 0, 0)
    absorb(0, 0, 0)
    b = routes.me
    for s in range(SLOTS):
        for h in range(2):
            lanes = slice(h * HALF, h * HALF + HALF)
            degrees = b * WIDTH + h * HALF + lane_iota((4, HALF))
            keep = degrees >= jnp.maximum(ids_ref[s], 2)
            refined[s, :, lanes] = jnp.where(keep, harm_ref[s, :, lanes] + update[h, b, s], 0.0)
    for h, full, b, target in started:
        each_cut(b, lambda c: copy(h, full, b, target, c).wait_send())


def adjoint_scatter(order_ids, legendre, harmonics, returned):
    legs = 2 * len(LEGS)
    vmem = pl.BlockSpec(memory_space=pltpu.VMEM)
    return pl.pallas_call(
        adjoint_scatter_kernel,
        out_shape=jax.ShapeDtypeStruct(harmonics.shape, F32),
        in_specs=[
            pl.BlockSpec(memory_space=pltpu.SMEM),
            pl.BlockSpec(memory_space=pl.ANY),
            vmem,
            vmem,
        ],
        out_specs=vmem,
        scratch_shapes=[
            pltpu.VMEM(legendre.shape, F32),
            pltpu.VMEM((2, BLOCKS, SLOTS, 4, HALF), F32),
            pltpu.VMEM((legs, SLOTS, 4, HALF), F32),
            pltpu.VMEM((SLOTS, 8, 8, LANES), F32),
            pltpu.SemaphoreType.DMA((SLOTS,)),
            pltpu.SemaphoreType.DMA((legs * CUTS,)),
            pltpu.SemaphoreType.DMA((legs * CUTS,)),
        ],
        compiler_params=pltpu.CompilerParams(
            collective_id=2, has_side_effects=True, vmem_limit_bytes=VMEM_LIMIT
        ),
        name="adjoint_scatter",
    )(order_ids, legendre, harmonics, returned)


def to_rows(sky):
    cycles = sky.shape[0]
    parts = sky.reshape(cycles, 2, LANES, LANES)
    return jnp.transpose(parts, (0, 2, 1, 3)).reshape(cycles, 2 * LANES, LANES)


def from_rows(rows):
    cycles = rows.shape[0]
    parts = rows.reshape(cycles, LANES, 2, LANES)
    return jnp.transpose(parts, (0, 2, 1, 3)).reshape(cycles, 2, LANES * LANES)


def body(harmonics, legendre, sky_map, cycle_length, cycle_offset, cycle_weight, order_ids):
    scale = math.sqrt(8192 * 128 / 4194304)
    message = gather_forward(order_ids, legendre, harmonics)
    rows, returned = pixel_phase(
        scale, cycle_length, cycle_offset, cycle_weight, message, to_rows(sky_map)
    )
    refined = adjoint_scatter(order_ids, legendre, harmonics, returned)
    return refined, from_rows(rows)


def solution(mesh):
    return jax.shard_map(
        body,
        mesh=mesh,
        in_specs=(
            P("order", None, "blk"),
            P("order", None, "blk", None),
            P(("blk", "order"), None, None),
            P(("blk", "order")),
            P(("blk", "order")),
            P(("blk", "order")),
            P("order"),
        ),
        out_specs=(P("order", None, "blk"), P(("blk", "order"), None, None)),
        check_vma=False,
    )
```

time: 183 us -> 71.8 us (0.39)
  waiting for transfers between devices: 123 us -> 0 us
  Pallas kernels: 20.6 us -> 68.7 us
  blocking collectives: 19.6 us -> 0 us
  between operations: 14.1 us -> 0.66 us
  local copies, waits for them, and re-layouts: 4.93 us -> 2.28 us
    unnamed x3 -> x0, waiting for transfers between devices: 72.9 us -> none
    all_gather x1 -> x0, waiting for transfers between devices: 49.7 us -> none  [body(): gathered = lax.all_gather(harmonics, 'blk', axis=0)]
    pallas_call x2, Pallas kernels: 16.5 us -> 54 us  [the longest x1 27.4 us: gather_forward(): pl.pallas_call(gather_forward_kernel, out_shape=jax.ShapeDtypeStruct((128...]
    all_to_all x2 -> x0, blocking collectives: 19.6 us -> none  [body(): lax.all_to_all(message.reshape(GROUP, 16, LANES), 'order', split_axis=0,...]
    pallas_call x1, Pallas kernels: 4.04 us -> 14.7 us  [pixel_phase(): pl.pallas_call(functools.partial(pixel_kernel, scale), out_shape=(jax.Sha...]
    pallas_call x1 -> x0, local copies, waits for them, and re-layouts: 3.57 us -> none  [adjoint(): pl.pallas_call(adjoint_kernel, out_shape=jax.ShapeDtypeStruct((BLOCKS, SL...]
  transfers between devices with their start and end apart: 2 -> 0, of which waited for: 2 -> 0; matrix products, arithmetic and copies ran while one was open for 0% -> 0% of each run, Pallas kernels for 0% -> 0%
where the time goes in v2:
time: 71.8 us; the launch traced here: 71.6 us
  Pallas kernels  68.7 us (96%)
  local copies, waits for them, and re-layouts  2.28 us (3%)
    pallas_call x1, Pallas kernels, gather_forward(): pl.pallas_call(gather_forward_kernel, out_shape=jax.ShapeDtypeStruct((128...  27.4 us
    pallas_call x1, Pallas kernels, adjoint_scatter(): pl.pallas_call(adjoint_scatter_kernel, out_shape=jax.ShapeDtypeStruct(har...  26.6 us
    pallas_call x1, Pallas kernels, pixel_phase(): pl.pallas_call(functools.partial(pixel_kernel, scale), out_shape=(jax.Sha...  14.7 us
    unnamed x4, local copies, waits for them, and re-layouts  2.28 us

profile of v2, /device:TPU:0, one launch (start us, length us, event | category | flops | bytes accessed | tf_op | source)
XLA Modules:
  0.0 71.6 jit_solution(16298856530549709547)
XLA Ops:
  0.6 27.4 %gather_forward.1.message = f32[128,128]{1,0:T(8,128)} custom-call(s32[16]{0:T(128)} %ids_ref.3, f32[16,2,16,8192]{3,2,1,0:T(8,128)} %leg_ref.3, f32[16,4,512]{2,1,0:T(4,128)} %harm_ref.3), custom_call_target="tpu_custom_call" | custom-call | tf_op jit(solution)/shard_map/gather_forward/pallas_call | solution.py:254
  28.0 14.7 %pixel_phase.1 = (f32[2,256,128]{2,1,0:T(8,128)}, f32[128,128]{1,0:T(8,128)}) custom-call(s32[2]{0:T(128)} %length.1, s32[2]{0:T(128)} %offset.1, f32[2]{0:T(128)} %weight.1, f32[128,128]{1,0:T(8,128)} %gather_forward.1.message, f32[2,256,128]{2,1,0:T(8,128)} %bitcast.10), custom_call_target="tpu_custom_call" | custom-call | tf_op jit(solution)/shard_map/pixel_phase/pallas_call | solution.py:415
  42.7 0.0 copy-start
  42.7 26.6 %adjoint_scatter.1 = f32[16,4,512]{2,1,0:T(4,128)} custom-call(s32[16]{0:T(128)} %ids_ref.3, f32[16,2,16,8192]{3,2,1,0:T(8,128)} %leg_ref.3, f32[16,4,512]{2,1,0:T(4,128)} %harm_ref.3, f32[128,128]{1,0:T(8,128)} %get-tuple-element.4.returned), custom_call_target="tpu_custom_call" | custom-call | tf_op jit(solution)/shard_map/adjoint_scatter/pallas_call | solution.py:582
  69.4 1.6 %copy.13 = f32[16,4,512]{2,1,0:T(4,128)} copy(f32[16,4,512]{2,1,0:T(4,128)} %adjoint_scatter.1) | data formatting | bytes 262144
  70.9 0.0 copy-done
  70.9 0.7 copy.14
Async XLA Ops:
  42.7 28.2 %copy-start = (f32[2,256,128]{2,1,0:T(8,128)S(1)}, f32[2,256,128]{2,1,0:T(8,128)}, u32[]{:S(2)}) copy-start(f32[2,256,128]{2,1,0:T(8,128)} %get-tuple-element.5) | copy-start | bytes 786436
